TPU v7x, 32 devices: a whole 2x2x4 slice. The times are simulated.
32 devices in a mesh: dp: 4 (over y, x), expert: 4 (over z), tensor: 2 (over core).
Axes of the slice: x: 2, y: 2, z: 4, core: 2. Of those that a mesh axis runs over, the one named last changes fastest.
Arguments:
- tokens: bfloat16 [4096, 2048], P(('dp', 'expert')), may hold values from -6 to 6
- segments: int32 [4, 1024], P('dp', 'expert'), may hold values from 0 to 7, never falling along the last dimension, each value on 1 to 512 neighbouring positions
- routes: int32 [4096, 4], P(('dp', 'expert')), may hold values from 0 to 7, all different within a row; in each aligned block of 256 rows (0 to 255, 256 to 511, ...) at most 192 rows name the same one
- norm1_gain: bfloat16 [2048], replicated, may hold values from 0.5 to 1.5
- q_weight: bfloat16 [2048, 2048], P(None, 'tensor'), may hold values from -0.125 to 0.125
- k_weight: bfloat16 [2048, 2048], P(None, 'tensor'), may hold values from -0.125 to 0.125
- v_weight: bfloat16 [2048, 2048], P(None, 'tensor'), may hold values from -0.125 to 0.125
- o_weight: bfloat16 [2048, 2048], P(None, 'tensor'), may hold values from -0.5 to 0.5
- norm2_gain: bfloat16 [2048], replicated, may hold values from 0.5 to 1.5
- router_weight: bfloat16 [2048, 8], replicated, may hold values from -0.0625 to 0.0625
- shared_gate_vector: bfloat16 [2048], replicated, may hold values from -0.125 to 0.125
- shared_gate_weight: bfloat16 [2048, 5632], P(None, 'tensor'), may hold values from -0.125 to 0.125
- shared_up_weight: bfloat16 [2048, 5632], P(None, 'tensor'), may hold values from -0.125 to 0.125
- shared_down_weight: bfloat16 [2048, 5632], P(None, 'tensor'), may hold values from -0.25 to 0.25
- expert_gate_weight: bfloat16 [8, 2048, 1408], P('expert', None, 'tensor'), may hold values from -0.125 to 0.125
- expert_up_weight: bfloat16 [8, 2048, 1408], P('expert', None, 'tensor'), may hold values from -0.125 to 0.125
- expert_down_weight: bfloat16 [8, 2048, 1408], P('expert', None, 'tensor'), may hold values from -1 to 1
- out_grad: bfloat16 [4096, 2048], P(('dp', 'expert')), may hold values from -6 to 6
Outputs:
- layer_out: float32 [4096, 2048], P(('dp', 'expert'))
- input_grad: float32 [4096, 2048], P(('dp', 'expert'))
- rms_stats: float32 [2, 4096], P(None, ('dp', 'expert'))
- norm1_gain_grad: float32 [2048], P(('dp', 'expert'))
- q_weight_grad: float32 [2048, 2048], P(('dp', 'expert'), 'tensor')
- k_weight_grad: float32 [2048, 2048], P(('dp', 'expert'), 'tensor')
- v_weight_grad: float32 [2048, 2048], P(('dp', 'expert'), 'tensor')
- o_weight_grad: float32 [2048, 2048], P(('dp', 'expert'), 'tensor')
- norm2_gain_grad: float32 [2048], P(('dp', 'expert'))
- router_grad: float32 [2048, 8], P(('dp', 'expert'))
- shared_vector_grad: float32 [2048], P(('dp', 'expert'))
- shared_gate_grad: float32 [2048, 5632], P(('dp', 'expert'), 'tensor')
- shared_up_grad: float32 [2048, 5632], P(('dp', 'expert'), 'tensor')
- shared_down_grad: float32 [2048, 5632], P(('dp', 'expert'), 'tensor')
- expert_gate_grad: float32 [8, 2048, 1408], P('expert', 'dp', 'tensor')
- expert_up_grad: float32 [8, 2048, 1408], P('expert', 'dp', 'tensor')
- expert_down_grad: float32 [8, 2048, 1408], P('expert', 'dp', 'tensor')
Inputs may be any that keep to these rules, and one draw needn't show every extreme that they name: `segments`: document numbers never fall along a sequence; each of the 8 documents of a sequence is present and holds 1 to 512 tokens, one exactly 512. `routes`: the 4 experts of a token differ. Among the 256 tokens of one index of dp and expert, no expert is named more than 192 times, a bound that some block reaches.
All inputs are finite; a program needn't handle non-finite values.
Results may differ from a plain program's by a relative error of at most 0.02.
Values may be sent and summed in bfloat16 or wider, within the bound.
A program may use at most 384 MiB of HBM per device.

v0:
```python
import jax
import jax.numpy as jnp
from jax import lax
from jax.sharding import PartitionSpec as P

HD = 128
epsilon = 1e-06
precise = lax.Precision.HIGHEST


def norm_forward(values, gain):
    inverse = lax.rsqrt(jnp.mean(values * values, axis=-1, keepdims=True) + epsilon)
    return (values * inverse * gain, inverse)


def norm_backward(values, inverse, gain, upstream):
    scaled = upstream * gain
    gain_grad = jnp.sum(upstream * values * inverse, axis=0)
    inner = jnp.mean(scaled * values, axis=-1, keepdims=True)
    return (inverse * scaled - values * inverse * inverse * inverse * inner, gain_grad)


def silu_slope(values):
    sigma = jax.nn.sigmoid(values)
    return sigma * (1.0 + values * (1.0 - sigma))


def cross_rows(left, right):
    return lax.dot_general(
        left, right, (((0,), (0,)), ((), ())), preferred_element_type=jnp.float32
    )


def cross_cols(left, right):
    return lax.dot_general(
        left, right, (((1,), (1,)), ((), ())), preferred_element_type=jnp.float32
    )


def plain_dot(left, right):
    return jnp.dot(left, right, preferred_element_type=jnp.float32)


def body(
    tokens,
    segments,
    routes,
    norm1_gain,
    q_weight,
    k_weight,
    v_weight,
    o_weight,
    norm2_gain,
    router_weight,
    shared_gate_vector,
    shared_gate_weight,
    shared_up_weight,
    shared_down_weight,
    expert_gate_weight,
    expert_up_weight,
    expert_down_weight,
    out_grad,
):
    tok_rows = tokens.shape[0]
    feat_width = tokens.shape[1]
    local_count = expert_gate_weight.shape[0]
    expert_count = local_count * lax.axis_size("expert")
    top_count = routes.shape[1]
    slot_count = 3 * tok_rows * top_count // (2 * expert_count)
    head_count = q_weight.shape[1] // HD
    score_scale = HD ** (-0.5)
    first_norm_gain = norm1_gain.astype(jnp.float32)
    second_norm_gain = norm2_gain.astype(jnp.float32)
    input_rows = tokens.astype(jnp.float32)
    normed_one, inverse_one = norm_forward(input_rows, first_norm_gain)
    normed_low = normed_one.astype(jnp.bfloat16)
    queries = plain_dot(normed_low, q_weight).astype(jnp.bfloat16)
    own_keys = plain_dot(normed_low, k_weight).astype(jnp.bfloat16)
    own_values = plain_dot(normed_low, v_weight).astype(jnp.bfloat16)
    labels = segments.astype(jnp.bfloat16)
    all_keys, all_values, key_labels = (
        lax.all_gather(own_keys, "expert", axis=0, tiled=True),
        lax.all_gather(own_values, "expert", axis=0, tiled=True),
        lax.all_gather(labels, "expert", axis=1, tiled=True),
    )
    key_span = all_keys.shape[0]
    query_pos = lax.axis_index("expert") * tok_rows + jnp.arange(tok_rows)
    key_pos = jnp.arange(key_span)
    allowed = (key_pos[None, :] <= query_pos[:, None]) & (
        key_labels[0][None, :] == labels[0][:, None]
    )
    query_heads = queries.reshape(tok_rows, head_count, HD)
    key_heads = all_keys.reshape(key_span, head_count, HD)
    value_heads = all_values.reshape(key_span, head_count, HD)

    def masked_scores():
        raw_scores = (
            jnp.einsum("qhd,khd->hqk", query_heads, key_heads, preferred_element_type=jnp.float32)
            * score_scale
        )
        return jnp.where(allowed[None], raw_scores, -jnp.inf)

    scores = masked_scores()
    top_score = jnp.max(scores, axis=-1, keepdims=True)
    exponent = jnp.exp(scores - top_score)
    totals = jnp.sum(exponent, axis=-1, keepdims=True)
    log_total = top_score + jnp.log(totals)
    weights_low = (exponent / totals).astype(jnp.bfloat16)
    mixed_heads = jnp.einsum(
        "hqk,khd->qhd", weights_low, value_heads, preferred_element_type=jnp.float32
    )
    mixed_low = mixed_heads.reshape(tok_rows, -1).astype(jnp.bfloat16)
    residual_state = input_rows + lax.psum(
        cross_cols(mixed_low, o_weight).astype(jnp.bfloat16), "tensor"
    ).astype(jnp.float32)
    normed_two, inverse_two = norm_forward(residual_state, second_norm_gain)
    routed_in = normed_two.astype(jnp.bfloat16)
    router_probs = jax.nn.softmax(plain_dot(routed_in, router_weight), axis=-1)
    chosen = routes[:, :, None] == jnp.arange(expert_count)[None, None, :]
    gate_values = jnp.sum(jnp.where(chosen, router_probs[:, None, :], 0.0), axis=-1)
    shared_gate_pre = plain_dot(routed_in, shared_gate_weight)
    shared_up_pre = plain_dot(routed_in, shared_up_weight)
    shared_hidden = (jax.nn.silu(shared_gate_pre) * shared_up_pre).astype(jnp.bfloat16)
    shared_out = cross_cols(shared_hidden, shared_down_weight)
    shared_sigma = jax.nn.sigmoid(plain_dot(routed_in, shared_gate_vector))
    flat_routes = routes.reshape(-1)
    route_hot = (flat_routes[:, None] == jnp.arange(expert_count)[None, :]).astype(jnp.int32)
    slot_index = jnp.sum((jnp.cumsum(route_hot, axis=0) - 1) * route_hot, axis=1)
    placement = flat_routes * slot_count + slot_index
    assign_total = tok_rows * top_count
    owners = (
        jnp.full((expert_count * slot_count,), assign_total, jnp.int32)
        .at[placement]
        .set(jnp.arange(assign_total, dtype=jnp.int32))
    )
    padded_rows = jnp.concatenate([routed_in, jnp.zeros((1, feat_width), jnp.bfloat16)], axis=0)
    outgoing = padded_rows[owners // top_count].reshape(expert_count, 1, slot_count, feat_width)
    received = lax.all_to_all(outgoing, "expert", split_axis=0, concat_axis=1, tiled=True)
    gate_pre = jnp.einsum(
        "esmd,edf->esmf", received, expert_gate_weight, preferred_element_type=jnp.float32
    )
    up_pre = jnp.einsum(
        "esmd,edf->esmf", received, expert_up_weight, preferred_element_type=jnp.float32
    )
    expert_hidden = (jax.nn.silu(gate_pre) * up_pre).astype(jnp.bfloat16)
    result = jnp.einsum(
        "esmf,edf->esmd", expert_hidden, expert_down_weight, preferred_element_type=jnp.float32
    )
    returned = lax.all_to_all(
        result.astype(jnp.bfloat16), "expert", split_axis=1, concat_axis=0, tiled=True
    ).astype(result.dtype)
    picked = returned.reshape(expert_count * slot_count, feat_width)[placement].reshape(
        tok_rows, top_count, feat_width
    )
    routed_output = jnp.sum(gate_values[:, :, None] * picked, axis=1)
    branch_sum = lax.psum(
        (routed_output + shared_sigma[:, None] * shared_out).astype(jnp.bfloat16), "tensor"
    ).astype(jnp.float32)
    layer_out = residual_state + branch_sum
    upstream = out_grad.astype(jnp.float32)
    d_shared = (shared_sigma[:, None] * upstream).astype(jnp.bfloat16)
    d_sigma = jnp.sum(upstream * shared_out, axis=-1)
    d_shared_hidden = plain_dot(d_shared, shared_down_weight)
    d_shared_gate = (d_shared_hidden * shared_up_pre * silu_slope(shared_gate_pre)).astype(
        jnp.bfloat16
    )
    d_shared_up = (d_shared_hidden * jax.nn.silu(shared_gate_pre)).astype(jnp.bfloat16)
    grad_shared_gate = cross_rows(routed_in, d_shared_gate)
    grad_shared_up = cross_rows(routed_in, d_shared_up)
    grad_shared_down = cross_rows(d_shared, shared_hidden)
    d_routed = cross_cols(d_shared_gate, shared_gate_weight) + cross_cols(
        d_shared_up, shared_up_weight
    )
    d_gates = jnp.sum(upstream[:, None, :] * picked, axis=-1)
    d_expert_out = (
        (gate_values[:, :, None] * upstream[:, None, :])
        .astype(jnp.bfloat16)
        .reshape(assign_total, feat_width)
    )
    padded_grads = jnp.concatenate([d_expert_out, jnp.zeros((1, feat_width), jnp.bfloat16)], axis=0)
    grads_out = padded_grads[owners].reshape(expert_count, 1, slot_count, feat_width)
    incoming = lax.all_to_all(grads_out, "expert", split_axis=0, concat_axis=1, tiled=True)
    expert_hidden = (jax.nn.silu(gate_pre) * up_pre).astype(jnp.bfloat16)
    d_hidden = jnp.einsum(
        "esmd,edf->esmf", incoming, expert_down_weight, preferred_element_type=jnp.float32
    )
    d_gate_pre = (d_hidden * up_pre * silu_slope(gate_pre)).astype(jnp.bfloat16)
    d_up_pre = (d_hidden * jax.nn.silu(gate_pre)).astype(jnp.bfloat16)
    d_rows = jnp.einsum(
        "esmf,edf->esmd", d_gate_pre, expert_gate_weight, preferred_element_type=jnp.float32
    )
    d_rows = d_rows + jnp.einsum(
        "esmf,edf->esmd", d_up_pre, expert_up_weight, preferred_element_type=jnp.float32
    )
    d_back = lax.all_to_all(
        d_rows.astype(jnp.bfloat16), "expert", split_axis=1, concat_axis=0, tiled=True
    ).astype(d_rows.dtype)
    grad_expert_gate = jnp.einsum(
        "esmd,esmf->edf", received, d_gate_pre, preferred_element_type=jnp.float32
    )
    grad_expert_up = jnp.einsum(
        "esmd,esmf->edf", received, d_up_pre, preferred_element_type=jnp.float32
    )
    grad_expert_down = jnp.einsum(
        "esmd,esmf->edf", incoming, expert_hidden, preferred_element_type=jnp.float32
    )
    sum_gate, sum_up, sum_down = (
        lax.psum_scatter(
            grad_expert_gate.astype(jnp.bfloat16), "dp", scatter_dimension=1, tiled=True
        ).astype(jnp.float32),
        lax.psum_scatter(
            grad_expert_up.astype(jnp.bfloat16), "dp", scatter_dimension=1, tiled=True
        ).astype(jnp.float32),
        lax.psum_scatter(
            grad_expert_down.astype(jnp.bfloat16), "dp", scatter_dimension=1, tiled=True
        ).astype(jnp.float32),
    )
    back_rows = d_back.reshape(expert_count * slot_count, feat_width)[placement].reshape(
        tok_rows, top_count, feat_width
    )
    d_routed = d_routed + jnp.sum(back_rows, axis=1)
    d_probs = jnp.sum(jnp.where(chosen, d_gates[:, :, None], 0.0), axis=1)
    d_logits = router_probs * (d_probs - jnp.sum(router_probs * d_probs, axis=-1, keepdims=True))
    d_vector = d_sigma * shared_sigma * (1.0 - shared_sigma)
    router_matrix = router_weight.astype(jnp.float32)
    gate_vector_weight = shared_gate_vector.astype(jnp.float32)
    d_routed = (
        d_routed
        + jnp.dot(d_logits, router_matrix.T, precision=precise)
        + d_vector[:, None] * gate_vector_weight[None, :]
    )
    d_normed_two, d_logits, d_vector = (
        lax.psum(d_routed.astype(jnp.bfloat16), "tensor").astype(jnp.float32),
        lax.psum(d_logits.astype(jnp.bfloat16), "tensor").astype(jnp.float32),
        lax.psum(d_vector.astype(jnp.bfloat16), "tensor").astype(jnp.float32),
    )
    grad_router = jnp.dot(
        routed_in.T, d_logits, precision=precise, preferred_element_type=jnp.float32
    )
    grad_vector = jnp.dot(
        routed_in.T, d_vector, precision=precise, preferred_element_type=jnp.float32
    )
    d_hidden_norm, grad_norm_two = norm_backward(
        residual_state, inverse_two, second_norm_gain, d_normed_two
    )
    d_state = upstream + d_hidden_norm
    d_state_low = d_state.astype(jnp.bfloat16)
    d_mixed = plain_dot(d_state_low, o_weight).astype(jnp.bfloat16)
    grad_out_proj = cross_rows(d_state_low, mixed_low)
    probs_full = jnp.exp(masked_scores() - log_total)
    probs_low = probs_full.astype(jnp.bfloat16)
    d_mixed_heads = d_mixed.reshape(tok_rows, head_count, HD)
    d_value_all = jnp.einsum(
        "hqk,qhd->khd", probs_low, d_mixed_heads, preferred_element_type=jnp.float32
    )
    d_probs_att = jnp.einsum(
        "qhd,khd->hqk", d_mixed_heads, value_heads, preferred_element_type=jnp.float32
    )
    d_scores = (
        probs_full * (d_probs_att - jnp.sum(probs_full * d_probs_att, axis=-1, keepdims=True))
    ).astype(jnp.bfloat16)
    d_queries = (
        (
            jnp.einsum("hqk,khd->qhd", d_scores, key_heads, preferred_element_type=jnp.float32)
            * score_scale
        )
        .reshape(tok_rows, -1)
        .astype(jnp.bfloat16)
    )
    d_key_all = (
        jnp.einsum("hqk,qhd->khd", d_scores, query_heads, preferred_element_type=jnp.float32)
        * score_scale
    )
    d_keys, d_values = (
        lax.psum_scatter(
            d_key_all.reshape(key_span, -1).astype(jnp.bfloat16),
            "expert",
            scatter_dimension=0,
            tiled=True,
        ).astype(jnp.float32),
        lax.psum_scatter(
            d_value_all.reshape(key_span, -1).astype(jnp.bfloat16),
            "expert",
            scatter_dimension=0,
            tiled=True,
        ).astype(jnp.float32),
    )
    d_keys_low = d_keys.astype(jnp.bfloat16)
    d_values_low = d_values.astype(jnp.bfloat16)
    grad_query = cross_rows(normed_low, d_queries)
    grad_key = cross_rows(normed_low, d_keys_low)
    grad_value = cross_rows(normed_low, d_values_low)
    d_normed_one = (
        cross_cols(d_queries, q_weight)
        + cross_cols(d_keys_low, k_weight)
        + cross_cols(d_values_low, v_weight)
    )
    d_normed_one = lax.psum(d_normed_one.astype(jnp.bfloat16), "tensor").astype(jnp.float32)
    d_input_norm, grad_norm_one = norm_backward(
        input_rows, inverse_one, first_norm_gain, d_normed_one
    )
    input_grad = d_state + d_input_norm
    stats = jnp.concatenate([inverse_one.T, inverse_two.T], axis=0)
    g_one, g_query, g_key, g_value, g_out, g_two, g_router, g_vector, g_sgate, g_sup, g_sdown = (
        lax.psum_scatter(grad_norm_one, ("dp", "expert"), scatter_dimension=0, tiled=True),
        lax.psum_scatter(grad_query, ("dp", "expert"), scatter_dimension=0, tiled=True),
        lax.psum_scatter(grad_key, ("dp", "expert"), scatter_dimension=0, tiled=True),
        lax.psum_scatter(grad_value, ("dp", "expert"), scatter_dimension=0, tiled=True),
        lax.psum_scatter(grad_out_proj, ("dp", "expert"), scatter_dimension=0, tiled=True),
        lax.psum_scatter(grad_norm_two, ("dp", "expert"), scatter_dimension=0, tiled=True),
        lax.psum_scatter(grad_router, ("dp", "expert"), scatter_dimension=0, tiled=True),
        lax.psum_scatter(grad_vector, ("dp", "expert"), scatter_dimension=0, tiled=True),
        lax.psum_scatter(grad_shared_gate, ("dp", "expert"), scatter_dimension=0, tiled=True),
        lax.psum_scatter(grad_shared_up, ("dp", "expert"), scatter_dimension=0, tiled=True),
        lax.psum_scatter(grad_shared_down, ("dp", "expert"), scatter_dimension=0, tiled=True),
    )
    return (
        layer_out,
        input_grad,
        stats,
        g_one,
        g_query,
        g_key,
        g_value,
        g_out,
        g_two,
        g_router,
        g_vector,
        g_sgate,
        g_sup,
        g_sdown,
        sum_gate,
        sum_up,
        sum_down,
    )


def solution(mesh):
    placed = (
        P(("dp", "expert"), None),
        P("dp", "expert"),
        P(("dp", "expert"), None),
        P(),
        P(None, "tensor"),
        P(None, "tensor"),
        P(None, "tensor"),
        P(None, "tensor"),
        P(),
        P(),
        P(),
        P(None, "tensor"),
        P(None, "tensor"),
        P(None, "tensor"),
        P("expert", None, "tensor"),
        P("expert", None, "tensor"),
        P("expert", None, "tensor"),
        P(("dp", "expert"), None),
    )
    return jax.shard_map(
        body,
        mesh=mesh,
        in_specs=placed,
        out_specs=(
            P(("dp", "expert"), None),
            P(("dp", "expert"), None),
            P(None, ("dp", "expert")),
            P(("dp", "expert")),
            P(("dp", "expert"), "tensor"),
            P(("dp", "expert"), "tensor"),
            P(("dp", "expert"), "tensor"),
            P(("dp", "expert"), "tensor"),
            P(("dp", "expert")),
            P(("dp", "expert"), None),
            P(("dp", "expert")),
            P(("dp", "expert"), "tensor"),
            P(("dp", "expert"), "tensor"),
            P(("dp", "expert"), "tensor"),
            P("expert", "dp", "tensor"),
            P("expert", "dp", "tensor"),
            P("expert", "dp", "tensor"),
        ),
        check_vma=False,
    )
```

profile of v0, /device:TPU:0, one launch (start us, length us, event | category | flops | bytes accessed | tf_op | source)
XLA Modules:
  0.0 3415.2 jit_solution(6877648826485437788)
XLA Ops:
  23.5 12.7 all_gather.12
  37.2 25.9 all-gather.5.cloned.1.call-done
  74.6 35.3 %all-gather.3.cloned.1.call-done = bf16[1024,1024]{1,0:T(8,128)(2,1)} async-done(((bf16[256,1024]{1,0:T(8,128)(2,1)}), bf16[1024,1024]{1,0:T(8,128)(2,1)}) %all-gather.3.cloned.1.call-update) | async-done | bytes 2097168 | tf_op jit(solution)/shard_map/all_gather | solution.py:83
  109.9 6.2 fusion.75
  126.6 10.4 all-reduce.12.cloned.1.call-done
  141.0 7.1 gather_fusion
  148.1 5.4 all-to-all-start
  153.5 5.4 mul.338
  158.9 10.0 mul.339
  177.0 15.4 gather_fusion.2
  192.5 100.0 %all-to-all-done = bf16[8,1,192,2048]{3,2,1,0:T(8,128)(2,1)} async-done(((bf16[8,1,192,2048]{3,2,1,0:T(8,128)(2,1)}), bf16[8,1,192,2048]{3,2,1,0:T(8,128)(2,1)}, u32[]{:S(2)}, u32[]{:S(2)}) %all-to-all-start) | async-done | bytes 6291488 | tf_op jit(solution)/shard_map/all_to_all | solution.py:138
  292.4 5.4 all-to-all-start.2
  297.9 10.3 fusion.6
  308.2 127.8 %all-to-all-done.2 = bf16[8,1,192,2048]{3,2,1,0:T(8,128)(2,1)} async-done(((bf16[8,1,192,2048]{3,2,1,0:T(8,128)(2,1)}), bf16[8,1,192,2048]{3,2,1,0:T(8,128)(2,1)}, u32[]{:S(2)}, u32[]{:S(2)}) %all-to-all-start.2) | async-done | bytes 6291488 | tf_op jit(solution)/shard_map/all_to_all | solution.py:182
  436.0 11.0 fusion.4
  446.9 13.4 multiply_convert_fusion.3
  460.4 5.3 fusion.27
  469.0 5.7 all-to-all-start.1
  474.7 11.0 fusion.11
  485.7 10.0 add_convert_fusion
  498.9 113.4 %all-to-all-done.1 = bf16[2,4,192,2048]{3,2,0,1:T(8,128)(2,1)} async-done(((bf16[2,4,192,2048]{3,2,0,1:T(8,128)(2,1)}), bf16[2,4,192,2048]{3,2,0,1:T(8,128)(2,1)}, u32[]{:S(2)}, u32[]{:S(2)}) %all-to-all-start.1) | async-done | bytes 6291488 | tf_op jit(solution)/shard_map/all_to_all | solution.py:149
  612.3 5.3 all-to-all-start.3
  619.6 6.4 fusion.111
  626.1 10.3 multiply_convert_fusion.8
  641.4 7.2 multiply_convert_fusion.6
  648.6 9.3 fusion.112
  657.9 8.8 bitcast_convert_fusion.4
  666.7 13.7 gather_fusion.1
  680.5 10.0 reshape.289
  690.5 11.1 multiply_reduce_fusion.1
  701.8 53.4 %all-to-all-done.3 = bf16[2,4,192,2048]{3,2,0,1:T(8,128)(2,1)} async-done(((bf16[2,4,192,2048]{3,2,0,1:T(8,128)(2,1)}), bf16[2,4,192,2048]{3,2,0,1:T(8,128)(2,1)}, u32[]{:S(2)}, u32[]{:S(2)}) %all-to-all-start.3) | async-done | bytes 6291488 | tf_op jit(solution)/shard_map/all_to_all | solution.py:195
  755.2 8.8 bitcast_convert_fusion.3
  764.0 13.6 gather_fusion.3
  777.6 9.8 reshape.291
  787.4 8.6 reduce_sum.163
  796.1 8.5 fusion.44
  806.9 18.9 all-reduce.14.cloned.1.call-done
  833.9 6.1 multiply_reduce_fusion
  844.9 6.3 fusion.69
  851.3 11.0 bitcast_convert_fusion
  862.8 10.7 bitcast_convert_fusion.2
  873.6 10.7 bitcast_convert_fusion.1
  894.1 5.7 convolution_add_fusion.2
  899.7 36.4 %reduce-scatter.16.cloned.1.call-done = bf16[256,1024]{0,1:T(8,128)(2,1)} async-done(((bf16[1024,1024]{0,1:T(8,128)(2,1)}), bf16[256,1024]{0,1:T(8,128)(2,1)}) %reduce-scatter.16.cloned.1.call-update) | async-done | bytes 524304 | tf_op jit(solution)/shard_map/reduce_scatter | solution.py:281
  936.1 5.3 fusion.45
  944.9 7.4 fusion.81
  953.0 5.9 fusion.100
  958.9 5.8 fusion.96
  964.8 5.8 fusion.98
  970.8 11.0 fusion.84
  981.9 10.8 fusion.116
  992.8 10.9 fusion.115
  1009.7 63.3 %reduce-scatter.34.cloned.1.call-done = bf16[2,512,704]{1,2,0:T(8,128)(2,1)} async-done(((bf16[2,2048,704]{1,2,0:T(8,128)(2,1)}), bf16[2,512,704]{1,2,0:T(8,128)(2,1)}) %reduce-scatter.34.cloned.1.call-update) | async-done | bytes 1441808 | tf_op jit(solution)/shard_map/reduce_scatter | solution.py:208
  1076.4 65.5 %reduce-scatter.36.cloned.1.call-done = bf16[2,512,704]{1,2,0:T(8,128)(2,1)} async-done(((bf16[2,2048,704]{1,2,0:T(8,128)(2,1)}), bf16[2,512,704]{1,2,0:T(8,128)(2,1)}) %reduce-scatter.36.cloned.1.call-update) | async-done | bytes 1441808 | tf_op jit(solution)/shard_map/reduce_scatter | solution.py:211
  1145.2 20.8 all-reduce.16.cloned.1.call-done
  1167.9 77.4 %all-reduce.5 = (f32[2048]{0:T(1024)S(1)}, f32[2048]{0:T(1024)S(1)}, f32[2048]{0:T(1024)S(1)}) all-reduce(f32[2048]{0:T(1024)S(1)} %get-tuple-element.21, f32[2048]{0:T(1024)S(1)} %get-tuple-element.19, f32[2048]{0:T(1024)S(1)} %bitcast.206), channel_id=4, replica_groups=mesh['dp'=4,'expert'=4,'tensor'=2] {'dp','expert'}, use_global_device_ids=true, to_apply=%region_27.28.clone | all-reduce | flops 6144 | bytes 49152
  1247.0 5.8 fusion.56
  1252.8 174.7 %reduce-scatter.24.cloned.1.call-done = f32[128,1024]{1,0:T(8,128)} async-done(((f32[2048,1024]{1,0:T(8,128)}), f32[128,1024]{1,0:T(8,128)}) %reduce-scatter.24.cloned.1.call-update) | async-done | bytes 524304 | tf_op jit(solution)/shard_map/reduce_scatter | solution.py:309
  1427.5 182.7 %reduce-scatter.18.cloned.1.call-done = f32[128,1024]{1,0:T(8,128)} async-done(((f32[2048,1024]{1,0:T(8,128)}), f32[128,1024]{1,0:T(8,128)}) %reduce-scatter.18.cloned.1.call-update) | async-done | bytes 524304 | tf_op jit(solution)/shard_map/reduce_scatter | solution.py:306
  1610.2 182.6 %reduce-scatter.22.cloned.1.call-done = f32[128,1024]{1,0:T(8,128)} async-done(((f32[2048,1024]{1,0:T(8,128)}), f32[128,1024]{1,0:T(8,128)}) %reduce-scatter.22.cloned.1.call-update) | async-done | bytes 524304 | tf_op jit(solution)/shard_map/reduce_scatter | solution.py:308
  1792.8 182.6 %reduce-scatter.20.cloned.1.call-done = f32[128,1024]{1,0:T(8,128)} async-done(((f32[2048,1024]{1,0:T(8,128)}), f32[128,1024]{1,0:T(8,128)}) %reduce-scatter.20.cloned.1.call-update) | async-done | bytes 524304 | tf_op jit(solution)/shard_map/reduce_scatter | solution.py:307
  1975.4 476.0 %reduce-scatter.32.cloned.1.call-done = f32[128,2816]{1,0:T(8,128)} async-done(((f32[2048,2816]{1,0:T(8,128)}), f32[128,2816]{1,0:T(8,128)}) %reduce-scatter.32.cloned.1.call-update) | async-done | bytes 1441808 | tf_op jit(solution)/shard_map/reduce_scatter | solution.py:315
  2451.3 478.4 %reduce-scatter.30.cloned.1.call-done = f32[128,2816]{1,0:T(8,128)} async-done(((f32[2048,2816]{1,0:T(8,128)}), f32[128,2816]{1,0:T(8,128)}) %reduce-scatter.30.cloned.1.call-update) | async-done | bytes 1441808 | tf_op jit(solution)/shard_map/reduce_scatter | solution.py:314
  2929.8 478.4 %reduce-scatter.28.cloned.1.call-done = f32[128,2816]{1,0:T(8,128)} async-done(((f32[2048,2816]{1,0:T(8,128)}), f32[128,2816]{1,0:T(8,128)}) %reduce-scatter.28.cloned.1.call-update) | async-done | bytes 1441808 | tf_op jit(solution)/shard_map/reduce_scatter | solution.py:313
  (247 shorter events, 110.6 us)
Async XLA Ops:
  7.2 161.7 %copy-start = (bf16[2048,8]{0,1:T(8,128)(2,1)S(1)}, bf16[2048,8]{0,1:T(8,128)(2,1)}, u32[]{:S(2)}) copy-start(bf16[2048,8]{0,1:T(8,128)(2,1)} %param.27) | copy-start | bytes 98308
  7.2 55.9 %all-gather.5.cloned.1.call-start = ((), (), s32[]{:S(2)}) async-start(), calls=%async_computation.18 | async-start | bytes 2621440 | tf_op jit(solution)/shard_map/all_gather | solution.py:82
  8.8 10.2 copy-start.27
  9.5 9.5 copy-start.18
  9.5 4.8 copy-start.2
  14.2 4.5 copy-start.46
  14.2 4.5 copy-start.33
  14.2 95.7 %all-gather.3.cloned.1.call-start = ((), (), s32[]{:S(2)}) async-start(), calls=%async_computation.17 | async-start | bytes 2621440 | tf_op jit(solution)/shard_map/all_gather | solution.py:83
  18.6 118.3 %all-reduce.12.cloned.1.call-start = ((), (), s32[]{:S(2)}) async-start(), calls=%async_computation.19 | async-start | bytes 2097152 | tf_op jit(solution)/shard_map/psum | solution.py:113
  69.4 40.5 %copy-start.31 = (f32[8,256]{1,0:T(8,128)}, f32[8,256]{1,0:T(8,128)S(1)}, u32[]{:S(2)}) copy-start(f32[8,256]{1,0:T(8,128)S(1)} %get-tuple-element.42) | copy-start | bytes 24580
  74.6 41.5 %copy-start.37 = (f32[8,256]{1,0:T(8,128)}, f32[8,256]{1,0:T(8,128)S(1)}, u32[]{:S(2)}) copy-start(f32[8,256]{1,0:T(8,128)S(1)} %fusion) | copy-start | bytes 24580
  109.9 6.2 copy-start.47
  118.6 22.3 copy-start.23
  140.9 485.1 %copy-start.4 = (bf16[256,2048]{1,0:T(8,128)(2,1)}, bf16[256,2048]{1,0:T(8,128)(2,1)S(1)}, u32[]{:S(2)}) copy-start(bf16[256,2048]{1,0:T(8,128)(2,1)S(1)} %multiply_convert_fusion.10) | copy-start | bytes 3145732
  148.1 5.4 copy-start.8
  148.1 144.3 %all-to-all-start = ((bf16[8,1,192,2048]{3,2,1,0:T(8,128)(2,1)}), bf16[8,1,192,2048]{3,2,1,0:T(8,128)(2,1)}, u32[]{:S(2)}, u32[]{:S(2)}) async-start(bf16[8,1,192,2048]{3,2,1,0:T(8,128)(2,1)} %bitcast.190), calls=%async_computation | async-start | bytes 12582912 | tf_op jit(solution)/shard_map/all_to_all | solution.py:138
  169.4 5.4 copy-start.39
  170.7 4.0 copy-start.20
  292.4 143.6 %all-to-all-start.2 = ((bf16[8,1,192,2048]{3,2,1,0:T(8,128)(2,1)}), bf16[8,1,192,2048]{3,2,1,0:T(8,128)(2,1)}, u32[]{:S(2)}, u32[]{:S(2)}) async-start(bf16[8,1,192,2048]{3,2,1,0:T(8,128)(2,1)} %bitcast.191), calls=%async_computation.2 | async-start | bytes 12582912 | tf_op jit(solution)/shard_map/all_to_all | solution.py:182
  436.0 24.4 slice-start.5
  446.9 13.4 slice-start.6
  460.4 5.3 copy-start.52
  469.0 143.3 %all-to-all-start.1 = ((bf16[2,4,192,2048]{3,2,0,1:T(8,128)(2,1)}), bf16[2,4,192,2048]{3,2,0,1:T(8,128)(2,1)}, u32[]{:S(2)}, u32[]{:S(2)}) async-start(bf16[2,4,192,2048]{3,2,0,1:T(8,128)(2,1)} %copy.121), calls=%async_computation.1 | async-start | bytes 12582912 | tf_op jit(solution)/shard_map/all_to_all | solution.py:149
  474.7 11.0 copy-start.51
  498.9 118.7 %copy-start.41 = (bf16[2048]{0:T(1024)(128)(2,1)S(1)}, bf16[2048]{0:T(1024)(128)(2,1)}, u32[]{:S(2)}) copy-start(bf16[2048]{0:T(1024)(128)(2,1)} %param.28) | copy-start | bytes 12292
  612.3 142.9 %all-to-all-start.3 = ((bf16[2,4,192,2048]{3,2,0,1:T(8,128)(2,1)}), bf16[2,4,192,2048]{3,2,0,1:T(8,128)(2,1)}, u32[]{:S(2)}, u32[]{:S(2)}) async-start(bf16[2,4,192,2048]{3,2,0,1:T(8,128)(2,1)} %copy.125), calls=%async_computation.3 | async-start | bytes 12582912 | tf_op jit(solution)/shard_map/all_to_all | solution.py:195
  617.6 208.2 %all-reduce.14.cloned.1.call-start = ((), (), s32[]{:S(2)}) async-start(), calls=%async_computation.20 | async-start | bytes 2097152 | tf_op jit(solution)/shard_map/psum | solution.py:233
  619.6 16.8 slice-start.2
  619.6 16.8 slice-start.3
  626.0 10.3 copy-start.50
  626.0 10.3 slice-start.4
  636.3 4.5 copy-start.17
  648.6 9.3 copy-start.16
  680.5 10.0 copy-start.13
  680.5 10.0 copy-start.21
  690.5 11.2 copy-start.34
  690.5 11.3 copy-start.26
  690.5 11.3 copy-start.40
  690.5 11.2 copy-start.43
  796.1 8.5 copy-start.30
  804.6 21.2 copy-start.3
  804.6 21.2 copy-start.9
  804.6 21.2 copy-start.24
  804.6 21.2 copy-start.36
  806.8 87.3 %reduce-scatter.14.cloned.1.call-start = ((), (), s32[]{:S(2)}) async-start(), calls=%async_computation.21 | async-start | bytes 2621440 | tf_op jit(solution)/shard_map/reduce_scatter | solution.py:275
  833.9 6.2 slice-start
  833.9 6.5 slice-start.1
  844.8 91.2 %reduce-scatter.16.cloned.1.call-start = ((), (), s32[]{:S(2)}) async-start(), calls=%async_computation.22 | async-start | bytes 2621440 | tf_op jit(solution)/shard_map/reduce_scatter | solution.py:281
  851.2 155.2 %reduce-scatter.38.cloned.1.call-start = ((), (), s32[]{:S(2)}) async-start(), calls=%async_computation.33 | async-start | bytes 7208960 | tf_op jit(solution)/shard_map/reduce_scatter | solution.py:214
  862.3 210.7 %reduce-scatter.34.cloned.1.call-start = ((), (), s32[]{:S(2)}) async-start(), calls=%async_computation.31 | async-start | bytes 7208960 | tf_op jit(solution)/shard_map/reduce_scatter | solution.py:208
  873.5 268.4 %reduce-scatter.36.cloned.1.call-start = ((), (), s32[]{:S(2)}) async-start(), calls=%async_computation.32 | async-start | bytes 7208960 | tf_op jit(solution)/shard_map/reduce_scatter | solution.py:211
  884.3 281.7 %all-reduce.16.cloned.1.call-start = ((), (), s32[]{:S(2)}) async-start(), calls=%async_computation.34 | async-start | bytes 4194304 | tf_op jit(solution)/shard_map/psum | solution.py:156
  884.5 3.6 copy-start.7
  899.7 41.8 %copy-start.45 = (bf16[256]{0:T(256)(128)(2,1)S(1)}, bf16[256]{0:T(256)(128)(2,1)}, u32[]{:S(2)}) copy-start(bf16[256]{0:T(256)(128)(2,1)} %get-tuple-element.30) | copy-start | bytes 1540
  899.7 44.3 %copy-start.5 = (bf16[256,2048]{1,0:T(8,128)(2,1)S(1)}, bf16[256,2048]{1,0:T(8,128)(2,1)}, u32[]{:S(2)}) copy-start(bf16[256,2048]{1,0:T(8,128)(2,1)} %copy-done.4) | copy-start | bytes 3145732
  941.4 311.4 %reduce-scatter.26.cloned.1.call-start = ((), (), s32[]{:S(2)}) async-start(), calls=%async_computation.27 | async-start | bytes 69632 | tf_op jit(solution)/shard_map/reduce_scatter | solution.py:311
  944.9 482.6 %reduce-scatter.24.cloned.1.call-start = ((), (), s32[]{:S(2)}) async-start(), calls=%async_computation.26 | async-start | bytes 8912896 | tf_op jit(solution)/shard_map/reduce_scatter | solution.py:309
  952.3 657.9 %reduce-scatter.18.cloned.1.call-start = ((), (), s32[]{:S(2)}) async-start(), calls=%async_computation.23 | async-start | bytes 8912896 | tf_op jit(solution)/shard_map/reduce_scatter | solution.py:306
  958.9 833.9 %reduce-scatter.22.cloned.1.call-start = ((), (), s32[]{:S(2)}) async-start(), calls=%async_computation.25 | async-start | bytes 8912896 | tf_op jit(solution)/shard_map/reduce_scatter | solution.py:308
  964.7 1010.6 %reduce-scatter.20.cloned.1.call-start = ((), (), s32[]{:S(2)}) async-start(), calls=%async_computation.24 | async-start | bytes 8912896 | tf_op jit(solution)/shard_map/reduce_scatter | solution.py:307
  970.6 1480.8 %reduce-scatter.32.cloned.1.call-start = ((), (), s32[]{:S(2)}) async-start(), calls=%async_computation.30 | async-start | bytes 24510464 | tf_op jit(solution)/shard_map/reduce_scatter | solution.py:315
  981.9 1947.9 %reduce-scatter.30.cloned.1.call-start = ((), (), s32[]{:S(2)}) async-start(), calls=%async_computation.29 | async-start | bytes 24510464 | tf_op jit(solution)/shard_map/reduce_scatter | solution.py:314
  992.7 2415.5 %reduce-scatter.28.cloned.1.call-start = ((), (), s32[]{:S(2)}) async-start(), calls=%async_computation.28 | async-start | bytes 24510464 | tf_op jit(solution)/shard_map/reduce_scatter | solution.py:313
  1076.4 170.6 %copy-start.10 = (bf16[256,2048]{1,0:T(8,128)(2,1)S(1)}, bf16[256,2048]{1,0:T(8,128)(2,1)}, u32[]{:S(2)}) copy-start(bf16[256,2048]{1,0:T(8,128)(2,1)} %all-reduce.12.cloned.1.call-done) | copy-start | bytes 3145732
  (18 other events, 33.5 us)
Sparse Core Ops, SparseCore 0:
  14.3 48.7 all-gather.4
  65.2 44.6 all-gather.2
  118.6 18.3 all-reduce.11
  806.9 18.8 all-reduce.13
  844.9 45.0 reduce-scatter.13
  892.9 43.1 reduce-scatter.15
  939.1 65.1 reduce-scatter.37
  1007.2 65.8 reduce-scatter.33
  1076.1 65.8 reduce-scatter.35
  1144.7 21.2 all-reduce.15
  1168.9 76.9 reduce-scatter.25
  1248.7 178.8 reduce-scatter.23
  1430.4 179.8 reduce-scatter.17
  1613.0 179.8 reduce-scatter.21
  1795.5 179.8 reduce-scatter.19
  1978.1 473.1 reduce-scatter.31
  2454.1 475.6 reduce-scatter.29
  2932.5 475.6 reduce-scatter.27
where the time goes:
time: 3430 us; the launch traced here: 3420 us
  waiting for transfers between devices  2830 us (83%)
  matrix products  262 us (8%)
  local copies, waits for them, and re-layouts  114 us (3%)
  blocking collectives  92.6 us (3%)
  other arithmetic  80.3 us (2%)
    reduce_scatter x1, waiting for transfers between devices, body(): lax.psum_scatter(grad_shared_gate, ('dp', 'expert'), scatter_dimension=0,...  478 us
    reduce_scatter x1, waiting for transfers between devices, body(): lax.psum_scatter(grad_shared_up, ('dp', 'expert'), scatter_dimension=0, t...  478 us
    reduce_scatter x1, waiting for transfers between devices, body(): lax.psum_scatter(grad_shared_down, ('dp', 'expert'), scatter_dimension=0,...  476 us
    reduce_scatter x1, waiting for transfers between devices, body(): lax.psum_scatter(grad_query, ('dp', 'expert'), scatter_dimension=0, tiled...  183 us
    reduce_scatter x1, waiting for transfers between devices, body(): lax.psum_scatter(grad_value, ('dp', 'expert'), scatter_dimension=0, tiled...  183 us
    reduce_scatter x1, waiting for transfers between devices, body(): lax.psum_scatter(grad_key, ('dp', 'expert'), scatter_dimension=0, tiled=T...  183 us
    reduce_scatter x1, waiting for transfers between devices, body(): lax.psum_scatter(grad_out_proj, ('dp', 'expert'), scatter_dimension=0, ti...  175 us
    all_to_all x1, waiting for transfers between devices, body(): lax.all_to_all(grads_out, 'expert', split_axis=0, concat_axis=1, tiled=True)  128 us
  transfers between devices with their start and end apart: 22, of which 19 were waited for; matrix products, arithmetic and copies ran while one was open for 9% of the time, Pallas kernels for 0%

commit v1 on v0

--- a/solution.py
+++ b/solution.py
@@ -146,8 +146,14 @@
     result = jnp.einsum(
         "esmf,edf->esmd", expert_hidden, expert_down_weight, preferred_element_type=jnp.float32
     )
-    returned = lax.all_to_all(
-        result.astype(jnp.bfloat16), "expert", split_axis=1, concat_axis=0, tiled=True
+    returned = jnp.concatenate(
+        lax.all_to_all(
+            jnp.stack(jnp.split(result.astype(jnp.bfloat16), lax.axis_size("expert"), axis=1)),
+            "expert",
+            0,
+            0,
+        ),
+        axis=0,
     ).astype(result.dtype)
     picked = returned.reshape(expert_count * slot_count, feat_width)[placement].reshape(
         tok_rows, top_count, feat_width

time: 3430 us -> 3430 us (level)
  no operation moved by 1% of the time
where the time goes in v1:
time: 3430 us; the launch traced here: 3420 us
  waiting for transfers between devices  2830 us (83%)
  matrix products  262 us (8%)
  local copies, waits for them, and re-layouts  112 us (3%)
  blocking collectives  92.6 us (3%)
  other arithmetic  83.5 us (2%)
    reduce_scatter x1, waiting for transfers between devices, body(): lax.psum_scatter(grad_shared_gate, ('dp', 'expert'), scatter_dimension=0,...  478 us
    reduce_scatter x1, waiting for transfers between devices, body(): lax.psum_scatter(grad_shared_up, ('dp', 'expert'), scatter_dimension=0, t...  478 us
    reduce_scatter x1, waiting for transfers between devices, body(): lax.psum_scatter(grad_shared_down, ('dp', 'expert'), scatter_dimension=0,...  476 us
    reduce_scatter x1, waiting for transfers between devices, body(): lax.psum_scatter(grad_query, ('dp', 'expert'), scatter_dimension=0, tiled...  183 us
    reduce_scatter x1, waiting for transfers between devices, body(): lax.psum_scatter(grad_value, ('dp', 'expert'), scatter_dimension=0, tiled...  183 us
    reduce_scatter x1, waiting for transfers between devices, body(): lax.psum_scatter(grad_key, ('dp', 'expert'), scatter_dimension=0, tiled=T...  183 us
    reduce_scatter x1, waiting for transfers between devices, body(): lax.psum_scatter(grad_out_proj, ('dp', 'expert'), scatter_dimension=0, ti...  175 us
    all_to_all x1, waiting for transfers between devices, body(): lax.all_to_all(grads_out, 'expert', split_axis=0, concat_axis=1, tiled=True)  128 us
  transfers between devices with their start and end apart: 22, of which 19 were waited for; matrix products, arithmetic and copies ran while one was open for 9% of the time, Pallas kernels for 0%

profile of v1, /device:TPU:0, one launch (start us, length us, event | category | flops | bytes accessed | tf_op | source)
XLA Modules:
  0.0 3416.4 jit_solution(10644620796815329896)
XLA Ops:
  23.5 12.7 all_gather.12
  37.2 25.9 all-gather.5.cloned.1.call-done
  74.6 35.3 %all-gather.3.cloned.1.call-done = bf16[1024,1024]{1,0:T(8,128)(2,1)} async-done(((bf16[256,1024]{1,0:T(8,128)(2,1)}), bf16[1024,1024]{1,0:T(8,128)(2,1)}) %all-gather.3.cloned.1.call-update) | async-done | bytes 2097168 | tf_op jit(solution)/shard_map/all_gather | solution.py:83
  109.9 6.2 fusion.75
  126.6 10.4 all-reduce.12.cloned.1.call-done
  141.0 7.1 gather_fusion
  148.1 5.4 all-to-all-start
  153.5 5.4 mul.338
  158.9 10.0 mul.339
  177.0 15.4 gather_fusion.2
  192.5 99.9 %all-to-all-done = bf16[8,1,192,2048]{3,2,1,0:T(8,128)(2,1)} async-done(((bf16[8,1,192,2048]{3,2,1,0:T(8,128)(2,1)}), bf16[8,1,192,2048]{3,2,1,0:T(8,128)(2,1)}, u32[]{:S(2)}, u32[]{:S(2)}) %all-to-all-start) | async-done | bytes 6291488 | tf_op jit(solution)/shard_map/all_to_all | solution.py:138
  292.4 5.5 all-to-all-start.2
  297.9 10.3 fusion.6
  308.2 127.7 %all-to-all-done.2 = bf16[8,1,192,2048]{3,2,1,0:T(8,128)(2,1)} async-done(((bf16[8,1,192,2048]{3,2,1,0:T(8,128)(2,1)}), bf16[8,1,192,2048]{3,2,1,0:T(8,128)(2,1)}, u32[]{:S(2)}, u32[]{:S(2)}) %all-to-all-start.2) | async-done | bytes 6291488 | tf_op jit(solution)/shard_map/all_to_all | solution.py:188
  435.9 10.9 fusion.4
  446.9 13.4 multiply_convert_fusion.3
  460.3 5.3 fusion.27
  470.0 5.7 all-to-all-start.1
  475.7 11.0 fusion.11
  486.7 10.0 add_convert_fusion
  499.9 113.4 %all-to-all-done.1 = bf16[4,2,1,192,2048]{4,3,1,2,0:T(8,128)(2,1)} async-done(((bf16[4,2,1,192,2048]{4,3,1,2,0:T(8,128)(2,1)}), bf16[4,2,1,192,2048]{4,3,1,2,0:T(8,128)(2,1)}, u32[]{:S(2)}, u32[]{:S(2)}) %all-to-all-start.1) | async-done | bytes 6291488 | tf_op jit(solution)/shard_map/all_to_all | solution.py:150
  613.3 5.2 all-to-all-start.3
  620.6 6.4 fusion.111
  627.1 10.3 multiply_convert_fusion.8
  642.4 7.2 multiply_convert_fusion.6
  649.6 9.3 fusion.112
  658.9 8.8 bitcast_convert_fusion.4
  667.8 13.8 gather_fusion.1
  681.5 10.0 reshape.288
  691.5 11.1 multiply_reduce_fusion.1
  702.8 53.4 %all-to-all-done.3 = bf16[2,4,192,2048]{3,2,0,1:T(8,128)(2,1)} async-done(((bf16[2,4,192,2048]{3,2,0,1:T(8,128)(2,1)}), bf16[2,4,192,2048]{3,2,0,1:T(8,128)(2,1)}, u32[]{:S(2)}, u32[]{:S(2)}) %all-to-all-start.3) | async-done | bytes 6291488 | tf_op jit(solution)/shard_map/all_to_all | solution.py:201
  756.2 8.8 bitcast_convert_fusion.3
  765.0 13.6 gather_fusion.3
  778.6 9.8 reshape.290
  788.5 8.6 reduce_sum.163
  797.1 8.5 fusion.44
  807.9 18.9 all-reduce.14.cloned.1.call-done
  835.0 6.1 multiply_reduce_fusion
  845.9 6.3 fusion.69
  852.3 11.0 bitcast_convert_fusion
  863.9 10.7 bitcast_convert_fusion.2
  874.7 10.7 bitcast_convert_fusion.1
  895.2 5.6 convolution_add_fusion.2
  900.8 36.4 %reduce-scatter.16.cloned.1.call-done = bf16[256,1024]{0,1:T(8,128)(2,1)} async-done(((bf16[1024,1024]{0,1:T(8,128)(2,1)}), bf16[256,1024]{0,1:T(8,128)(2,1)}) %reduce-scatter.16.cloned.1.call-update) | async-done | bytes 524304 | tf_op jit(solution)/shard_map/reduce_scatter | solution.py:287
  937.2 5.3 fusion.45
  946.0 7.3 fusion.81
  954.1 5.9 fusion.100
  960.0 5.8 fusion.96
  965.9 5.8 fusion.98
  971.9 11.0 fusion.84
  983.0 10.8 fusion.116
  993.9 10.9 fusion.115
  1010.8 63.3 %reduce-scatter.34.cloned.1.call-done = bf16[2,512,704]{1,2,0:T(8,128)(2,1)} async-done(((bf16[2,2048,704]{1,2,0:T(8,128)(2,1)}), bf16[2,512,704]{1,2,0:T(8,128)(2,1)}) %reduce-scatter.34.cloned.1.call-update) | async-done | bytes 1441808 | tf_op jit(solution)/shard_map/reduce_scatter | solution.py:214
  1077.5 65.5 %reduce-scatter.36.cloned.1.call-done = bf16[2,512,704]{1,2,0:T(8,128)(2,1)} async-done(((bf16[2,2048,704]{1,2,0:T(8,128)(2,1)}), bf16[2,512,704]{1,2,0:T(8,128)(2,1)}) %reduce-scatter.36.cloned.1.call-update) | async-done | bytes 1441808 | tf_op jit(solution)/shard_map/reduce_scatter | solution.py:217
  1146.3 20.8 all-reduce.16.cloned.1.call-done
  1169.0 77.4 %all-reduce.5 = (f32[2048]{0:T(1024)S(1)}, f32[2048]{0:T(1024)S(1)}, f32[2048]{0:T(1024)S(1)}) all-reduce(f32[2048]{0:T(1024)S(1)} %get-tuple-element.21, f32[2048]{0:T(1024)S(1)} %get-tuple-element.19, f32[2048]{0:T(1024)S(1)} %bitcast.216), channel_id=4, replica_groups=mesh['dp'=4,'expert'=4,'tensor'=2] {'dp','expert'}, use_global_device_ids=true, to_apply=%region_27.28.clone | all-reduce | flops 6144 | bytes 49152
  1248.1 5.8 fusion.56
  1253.9 174.7 %reduce-scatter.24.cloned.1.call-done = f32[128,1024]{1,0:T(8,128)} async-done(((f32[2048,1024]{1,0:T(8,128)}), f32[128,1024]{1,0:T(8,128)}) %reduce-scatter.24.cloned.1.call-update) | async-done | bytes 524304 | tf_op jit(solution)/shard_map/reduce_scatter | solution.py:315
  1428.6 182.7 %reduce-scatter.18.cloned.1.call-done = f32[128,1024]{1,0:T(8,128)} async-done(((f32[2048,1024]{1,0:T(8,128)}), f32[128,1024]{1,0:T(8,128)}) %reduce-scatter.18.cloned.1.call-update) | async-done | bytes 524304 | tf_op jit(solution)/shard_map/reduce_scatter | solution.py:312
  1611.3 182.6 %reduce-scatter.22.cloned.1.call-done = f32[128,1024]{1,0:T(8,128)} async-done(((f32[2048,1024]{1,0:T(8,128)}), f32[128,1024]{1,0:T(8,128)}) %reduce-scatter.22.cloned.1.call-update) | async-done | bytes 524304 | tf_op jit(solution)/shard_map/reduce_scatter | solution.py:314
  1793.9 182.6 %reduce-scatter.20.cloned.1.call-done = f32[128,1024]{1,0:T(8,128)} async-done(((f32[2048,1024]{1,0:T(8,128)}), f32[128,1024]{1,0:T(8,128)}) %reduce-scatter.20.cloned.1.call-update) | async-done | bytes 524304 | tf_op jit(solution)/shard_map/reduce_scatter | solution.py:313
  1976.5 476.0 %reduce-scatter.32.cloned.1.call-done = f32[128,2816]{1,0:T(8,128)} async-done(((f32[2048,2816]{1,0:T(8,128)}), f32[128,2816]{1,0:T(8,128)}) %reduce-scatter.32.cloned.1.call-update) | async-done | bytes 1441808 | tf_op jit(solution)/shard_map/reduce_scatter | solution.py:321
  2452.4 478.4 %reduce-scatter.30.cloned.1.call-done = f32[128,2816]{1,0:T(8,128)} async-done(((f32[2048,2816]{1,0:T(8,128)}), f32[128,2816]{1,0:T(8,128)}) %reduce-scatter.30.cloned.1.call-update) | async-done | bytes 1441808 | tf_op jit(solution)/shard_map/reduce_scatter | solution.py:320
  2930.9 478.4 %reduce-scatter.28.cloned.1.call-done = f32[128,2816]{1,0:T(8,128)} async-done(((f32[2048,2816]{1,0:T(8,128)}), f32[128,2816]{1,0:T(8,128)}) %reduce-scatter.28.cloned.1.call-update) | async-done | bytes 1441808 | tf_op jit(solution)/shard_map/reduce_scatter | solution.py:319
  (248 shorter events, 111.7 us)
Async XLA Ops:
  7.2 161.8 %copy-start = (bf16[2048,8]{0,1:T(8,128)(2,1)S(1)}, bf16[2048,8]{0,1:T(8,128)(2,1)}, u32[]{:S(2)}) copy-start(bf16[2048,8]{0,1:T(8,128)(2,1)} %param.27) | copy-start | bytes 98308
  7.2 55.9 %all-gather.5.cloned.1.call-start = ((), (), s32[]{:S(2)}) async-start(), calls=%async_computation.18 | async-start | bytes 2621440 | tf_op jit(solution)/shard_map/all_gather | solution.py:82
  8.8 10.2 copy-start.27
  9.5 9.5 copy-start.18
  9.5 4.8 copy-start.2
  14.2 4.5 copy-start.46
  14.2 4.5 copy-start.33
  14.2 95.7 %all-gather.3.cloned.1.call-start = ((), (), s32[]{:S(2)}) async-start(), calls=%async_computation.17 | async-start | bytes 2621440 | tf_op jit(solution)/shard_map/all_gather | solution.py:83
  18.6 118.3 %all-reduce.12.cloned.1.call-start = ((), (), s32[]{:S(2)}) async-start(), calls=%async_computation.19 | async-start | bytes 2097152 | tf_op jit(solution)/shard_map/psum | solution.py:113
  69.4 40.5 %copy-start.31 = (f32[8,256]{1,0:T(8,128)}, f32[8,256]{1,0:T(8,128)S(1)}, u32[]{:S(2)}) copy-start(f32[8,256]{1,0:T(8,128)S(1)} %get-tuple-element.46) | copy-start | bytes 24580
  74.6 41.5 %copy-start.37 = (f32[8,256]{1,0:T(8,128)}, f32[8,256]{1,0:T(8,128)S(1)}, u32[]{:S(2)}) copy-start(f32[8,256]{1,0:T(8,128)S(1)} %fusion) | copy-start | bytes 24580
  109.9 6.2 copy-start.47
  118.6 22.3 copy-start.23
  140.9 486.2 %copy-start.4 = (bf16[256,2048]{1,0:T(8,128)(2,1)}, bf16[256,2048]{1,0:T(8,128)(2,1)S(1)}, u32[]{:S(2)}) copy-start(bf16[256,2048]{1,0:T(8,128)(2,1)S(1)} %multiply_convert_fusion.10) | copy-start | bytes 3145732
  148.1 5.4 copy-start.8
  148.1 144.3 %all-to-all-start = ((bf16[8,1,192,2048]{3,2,1,0:T(8,128)(2,1)}), bf16[8,1,192,2048]{3,2,1,0:T(8,128)(2,1)}, u32[]{:S(2)}, u32[]{:S(2)}) async-start(bf16[8,1,192,2048]{3,2,1,0:T(8,128)(2,1)} %bitcast.200), calls=%async_computation | async-start | bytes 12582912 | tf_op jit(solution)/shard_map/all_to_all | solution.py:138
  169.4 5.4 copy-start.39
  170.7 4.0 copy-start.20
  292.4 143.5 %all-to-all-start.2 = ((bf16[8,1,192,2048]{3,2,1,0:T(8,128)(2,1)}), bf16[8,1,192,2048]{3,2,1,0:T(8,128)(2,1)}, u32[]{:S(2)}, u32[]{:S(2)}) async-start(bf16[8,1,192,2048]{3,2,1,0:T(8,128)(2,1)} %bitcast.201), calls=%async_computation.2 | async-start | bytes 12582912 | tf_op jit(solution)/shard_map/all_to_all | solution.py:188
  435.9 24.4 slice-start.5
  446.9 13.4 slice-start.6
  460.3 5.3 copy-start.52
  470.0 143.3 %all-to-all-start.1 = ((bf16[4,2,1,192,2048]{4,3,1,2,0:T(8,128)(2,1)}), bf16[4,2,1,192,2048]{4,3,1,2,0:T(8,128)(2,1)}, u32[]{:S(2)}, u32[]{:S(2)}) async-start(bf16[4,2,1,192,2048]{4,3,1,2,0:T(8,128)(2,1)} %pad_maximum_fusion), calls=%async_computation.1 | async-start | bytes 12582912 | tf_op jit(solution)/shard_map/all_to_all | solution.py:150
  475.7 11.0 copy-start.51
  499.9 118.7 %copy-start.41 = (bf16[2048]{0:T(1024)(128)(2,1)S(1)}, bf16[2048]{0:T(1024)(128)(2,1)}, u32[]{:S(2)}) copy-start(bf16[2048]{0:T(1024)(128)(2,1)} %param.28) | copy-start | bytes 12292
  613.3 142.9 %all-to-all-start.3 = ((bf16[2,4,192,2048]{3,2,0,1:T(8,128)(2,1)}), bf16[2,4,192,2048]{3,2,0,1:T(8,128)(2,1)}, u32[]{:S(2)}, u32[]{:S(2)}) async-start(bf16[2,4,192,2048]{3,2,0,1:T(8,128)(2,1)} %copy.136), calls=%async_computation.3 | async-start | bytes 12582912 | tf_op jit(solution)/shard_map/all_to_all | solution.py:201
  618.6 208.3 %all-reduce.14.cloned.1.call-start = ((), (), s32[]{:S(2)}) async-start(), calls=%async_computation.20 | async-start | bytes 2097152 | tf_op jit(solution)/shard_map/psum | solution.py:239
  620.6 16.8 slice-start.2
  620.6 16.8 slice-start.3
  627.0 10.3 copy-start.50
  627.0 10.3 slice-start.4
  637.3 4.5 copy-start.17
  649.6 9.3 copy-start.16
  681.5 10.0 copy-start.13
  681.5 10.0 copy-start.21
  691.5 11.2 copy-start.34
  691.5 11.3 copy-start.26
  691.5 11.3 copy-start.40
  691.5 11.2 copy-start.43
  797.1 8.5 copy-start.30
  805.6 21.2 copy-start.3
  805.6 21.2 copy-start.9
  805.6 21.2 copy-start.24
  805.6 21.2 copy-start.36
  807.8 87.3 %reduce-scatter.14.cloned.1.call-start = ((), (), s32[]{:S(2)}) async-start(), calls=%async_computation.21 | async-start | bytes 2621440 | tf_op jit(solution)/shard_map/reduce_scatter | solution.py:281
  834.9 6.2 slice-start
  835.0 6.5 slice-start.1
  845.9 91.3 %reduce-scatter.16.cloned.1.call-start = ((), (), s32[]{:S(2)}) async-start(), calls=%async_computation.22 | async-start | bytes 2621440 | tf_op jit(solution)/shard_map/reduce_scatter | solution.py:287
  852.3 155.2 %reduce-scatter.38.cloned.1.call-start = ((), (), s32[]{:S(2)}) async-start(), calls=%async_computation.33 | async-start | bytes 7208960 | tf_op jit(solution)/shard_map/reduce_scatter | solution.py:220
  863.4 210.8 %reduce-scatter.34.cloned.1.call-start = ((), (), s32[]{:S(2)}) async-start(), calls=%async_computation.31 | async-start | bytes 7208960 | tf_op jit(solution)/shard_map/reduce_scatter | solution.py:214
  874.6 268.4 %reduce-scatter.36.cloned.1.call-start = ((), (), s32[]{:S(2)}) async-start(), calls=%async_computation.32 | async-start | bytes 7208960 | tf_op jit(solution)/shard_map/reduce_scatter | solution.py:217
  885.4 281.7 %all-reduce.16.cloned.1.call-start = ((), (), s32[]{:S(2)}) async-start(), calls=%async_computation.34 | async-start | bytes 4194304 | tf_op jit(solution)/shard_map/psum | solution.py:162
  885.6 3.6 copy-start.7
  900.8 41.8 %copy-start.45 = (bf16[256]{0:T(256)(128)(2,1)S(1)}, bf16[256]{0:T(256)(128)(2,1)}, u32[]{:S(2)}) copy-start(bf16[256]{0:T(256)(128)(2,1)} %get-tuple-element.30) | copy-start | bytes 1540
  900.8 44.3 %copy-start.5 = (bf16[256,2048]{1,0:T(8,128)(2,1)S(1)}, bf16[256,2048]{1,0:T(8,128)(2,1)}, u32[]{:S(2)}) copy-start(bf16[256,2048]{1,0:T(8,128)(2,1)} %copy-done.4) | copy-start | bytes 3145732
  942.5 311.4 %reduce-scatter.26.cloned.1.call-start = ((), (), s32[]{:S(2)}) async-start(), calls=%async_computation.27 | async-start | bytes 69632 | tf_op jit(solution)/shard_map/reduce_scatter | solution.py:317
  946.0 482.6 %reduce-scatter.24.cloned.1.call-start = ((), (), s32[]{:S(2)}) async-start(), calls=%async_computation.26 | async-start | bytes 8912896 | tf_op jit(solution)/shard_map/reduce_scatter | solution.py:315
  953.4 657.9 %reduce-scatter.18.cloned.1.call-start = ((), (), s32[]{:S(2)}) async-start(), calls=%async_computation.23 | async-start | bytes 8912896 | tf_op jit(solution)/shard_map/reduce_scatter | solution.py:312
  960.0 833.9 %reduce-scatter.22.cloned.1.call-start = ((), (), s32[]{:S(2)}) async-start(), calls=%async_computation.25 | async-start | bytes 8912896 | tf_op jit(solution)/shard_map/reduce_scatter | solution.py:314
  965.8 1010.6 %reduce-scatter.20.cloned.1.call-start = ((), (), s32[]{:S(2)}) async-start(), calls=%async_computation.24 | async-start | bytes 8912896 | tf_op jit(solution)/shard_map/reduce_scatter | solution.py:313
  971.7 1480.8 %reduce-scatter.32.cloned.1.call-start = ((), (), s32[]{:S(2)}) async-start(), calls=%async_computation.30 | async-start | bytes 24510464 | tf_op jit(solution)/shard_map/reduce_scatter | solution.py:321
  983.0 1947.9 %reduce-scatter.30.cloned.1.call-start = ((), (), s32[]{:S(2)}) async-start(), calls=%async_computation.29 | async-start | bytes 24510464 | tf_op jit(solution)/shard_map/reduce_scatter | solution.py:320
  993.8 2415.5 %reduce-scatter.28.cloned.1.call-start = ((), (), s32[]{:S(2)}) async-start(), calls=%async_computation.28 | async-start | bytes 24510464 | tf_op jit(solution)/shard_map/reduce_scatter | solution.py:319
  1077.5 170.6 %copy-start.10 = (bf16[256,2048]{1,0:T(8,128)(2,1)S(1)}, bf16[256,2048]{1,0:T(8,128)(2,1)}, u32[]{:S(2)}) copy-start(bf16[256,2048]{1,0:T(8,128)(2,1)} %all-reduce.12.cloned.1.call-done) | copy-start | bytes 3145732
  (18 other events, 33.4 us)
Sparse Core Ops, SparseCore 0:
  14.3 48.7 all-gather.4
  65.2 44.6 all-gather.2
  118.6 18.3 all-reduce.11
  807.9 18.8 all-reduce.13
  846.0 45.0 reduce-scatter.13
  893.9 43.1 reduce-scatter.15
  940.2 65.1 reduce-scatter.37
  1008.3 65.8 reduce-scatter.33
  1077.2 65.8 reduce-scatter.35
  1145.8 21.2 all-reduce.15
  1170.0 76.9 reduce-scatter.25
  1249.8 178.8 reduce-scatter.23
  1431.5 179.8 reduce-scatter.17
  1614.1 179.8 reduce-scatter.21
  1796.6 179.8 reduce-scatter.19
  1979.2 473.1 reduce-scatter.31
  2455.2 475.6 reduce-scatter.29
  2933.6 475.6 reduce-scatter.27
